TPU v7x, 32 devices: a whole 2x2x4 slice. The times are simulated.
32 devices in a mesh: groups: 2 (over y), blk: 4 (over z), kv: 2 (over x), pair: 2 (over core).
Axes of the slice: x: 2, y: 2, z: 4, core: 2. Of those that a mesh axis runs over, the one named last changes fastest.
Arguments:
- queries: bfloat16 [128, 128, 128], P(('groups', 'blk'), ('kv', 'pair')), parts along dimension 0, may hold values from -15 to 15
- root_keys: bfloat16 [16384, 8, 128], P(('groups', 'blk', 'pair'), 'kv'), parts along dimension 0, may hold values from -4 to 4
- root_values: bfloat16 [16384, 8, 128], P(('groups', 'blk', 'pair'), 'kv'), parts along dimension 0, may hold values from -6 to 6
- branch_keys: bfloat16 [16, 2048, 8, 128], P(('groups', 'blk'), 'pair', 'kv'), parts along dimension 0, may hold values from -4 to 4
- branch_values: bfloat16 [16, 2048, 8, 128], P(('groups', 'blk'), 'pair', 'kv'), parts along dimension 0, may hold values from -6 to 6
- request_branch: int32 [128], P(('groups', 'blk')), parts along dimension 0, may hold values from 0 to 7, as said below
- seen_tokens: int32 [128], P(('groups', 'blk')), parts along dimension 0, may hold values from 1 to 2048, as said below
Outputs:
- attended: bfloat16 [128, 128, 128], P(('groups', 'blk'), ('kv', 'pair')), parts along dimension 0
There are 2 independent parts, one for each index of `groups`. A program takes and returns all parts, laid end to end along the dimension named above; each array names one. Nothing has to cross between parts.
Inputs may be any that keep to these rules, and one draw needn't show every extreme that they name: Within a part, request r belongs to one of the 2 branches stored on its own index of blk: request_branch[r] // 2 == r // 16, with r and the branch counted within the part. Every branch has at least one request. `seen_tokens`: on every index of blk some request sees all 2048 positions of its branch.
All inputs are finite; a program needn't handle non-finite values.
Results may differ from a plain program's by a relative error of at most 0.04.
Values may be sent and summed in bfloat16 or wider, within the bound.
A program may use at most 64 MiB of HBM per device.

v0:
```python
import math

import jax
import jax.numpy as jnp
from jax import lax
from jax.sharding import PartitionSpec as P

masked_floor = -1e30


def partner(value, axis, apart):
    return lax.ppermute(value, axis, [(i, i ^ 1 << apart) for i in range(lax.axis_size(axis))])


def combine_parts(first_part, second_part):
    sums_one, maxima_one, totals_one = first_part
    sums_two, maxima_two, totals_two = second_part
    largest = jnp.maximum(maxima_one, maxima_two)
    scale_one = jnp.exp(maxima_one - largest)
    scale_two = jnp.exp(maxima_two - largest)
    merged_sums = sums_one * scale_one[..., None] + sums_two * scale_two[..., None]
    return (merged_sums, largest, totals_one * scale_one + totals_two * scale_two)


def merge_sources(partials):
    sums, maxima, totals = partials
    largest = jnp.max(maxima, axis=0)
    factor = jnp.exp(maxima - largest[None])
    return (jnp.sum(sums * factor[..., None], axis=0), largest, jnp.sum(totals * factor, axis=0))


def pick_index(array_in, index_value, dim_index):
    return lax.dynamic_index_in_dim(array_in, index_value, dim_index, keepdims=False)


def local(queries, root_keys, root_values, branch_keys, branch_values, request_branch, seen_tokens):
    local_requests, local_heads, head_width = queries.shape
    root_tokens, shared_local, _ = root_keys.shape
    local_branches, half_tokens, _, _ = branch_keys.shape
    block_devices = lax.axis_size("blk")
    pair_devices = lax.axis_size("pair")
    shared_half = shared_local // pair_devices
    group_size = local_heads // shared_half
    row_count = local_requests * local_heads
    score_scale = 1.0 / math.sqrt(head_width)
    pair_index = lax.axis_index("pair")
    other_index = 1 - pair_index
    keys_split = root_keys.reshape(root_tokens, pair_devices, shared_half, head_width)
    values_split = root_values.reshape(root_tokens, pair_devices, shared_half, head_width)
    bkeys_split = branch_keys.reshape(
        local_branches, half_tokens, pair_devices, shared_half, head_width
    )
    bvalues_split = branch_values.reshape(
        local_branches, half_tokens, pair_devices, shared_half, head_width
    )
    received = partner(
        (
            pick_index(keys_split, other_index, 1),
            pick_index(values_split, other_index, 1),
            pick_index(bkeys_split, other_index, 2),
            pick_index(bvalues_split, other_index, 2),
        ),
        "pair",
        0,
    )
    keys_mine = jnp.concatenate([pick_index(keys_split, pair_index, 1), received[0]], axis=0)
    values_mine = jnp.concatenate([pick_index(values_split, pair_index, 1), received[1]], axis=0)
    bkeys_mine = jnp.concatenate([pick_index(bkeys_split, pair_index, 2), received[2]], axis=1)
    bvalues_mine = jnp.concatenate([pick_index(bvalues_split, pair_index, 2), received[3]], axis=1)
    gathered = lax.all_gather(queries, "blk", axis=0, tiled=True)
    query_blocks = gathered.reshape(
        block_devices, local_requests, shared_half, group_size, head_width
    )

    def root_partial_mine(query_block):
        scores = (
            jnp.einsum("rkgd,tkd->krgt", query_block, keys_mine, preferred_element_type=jnp.float32)
            * score_scale
        )
        maxima = jnp.max(scores, axis=-1)
        weights = jnp.exp(scores - maxima[..., None])
        totals = jnp.sum(weights, axis=-1)
        sums = jnp.einsum(
            "krgt,tkd->rkgd",
            weights.astype(jnp.bfloat16),
            values_mine,
            preferred_element_type=jnp.float32,
        )
        return (sums, jnp.transpose(maxima, (1, 0, 2)), jnp.transpose(totals, (1, 0, 2)))

    mine_sums, mine_maxima, mine_totals = lax.map(root_partial_mine, query_blocks)
    mine_sums = mine_sums.reshape(block_devices, row_count, head_width)
    mine_maxima = mine_maxima.reshape(block_devices, row_count)
    mine_totals = mine_totals.reshape(block_devices, row_count)
    merged = merge_sources(
        (
            lax.all_to_all(mine_sums, "blk", split_axis=0, concat_axis=0, tiled=True),
            lax.all_to_all(mine_maxima, "blk", split_axis=0, concat_axis=0, tiled=True),
            lax.all_to_all(mine_totals, "blk", split_axis=0, concat_axis=0, tiled=True),
        )
    )
    full_tokens = 2 * half_tokens
    key_count = local_branches * full_tokens
    keys_flat = bkeys_mine.reshape(key_count, shared_half, head_width)
    values_flat = bvalues_mine.reshape(key_count, shared_half, head_width)
    key_slot = jnp.arange(key_count, dtype=jnp.int32)
    within = key_slot % full_tokens
    position = jnp.where(
        within < half_tokens,
        pair_index * half_tokens + within,
        other_index * half_tokens + within - half_tokens,
    )
    visible = ((request_branch % local_branches)[:, None] == (key_slot // full_tokens)[None, :]) & (
        position[None, :] < seen_tokens[:, None]
    )
    visible_mask = visible[None, :, None, :]
    own_queries = queries.reshape(local_requests, shared_half, group_size, head_width)
    scores = (
        jnp.einsum("rkgd,tkd->krgt", own_queries, keys_flat, preferred_element_type=jnp.float32)
        * score_scale
    )
    scores = jnp.where(visible_mask, scores, masked_floor)
    maxima = jnp.max(scores, axis=-1)
    weights = jnp.where(visible_mask, jnp.exp(scores - maxima[..., None]), 0.0)
    totals = jnp.sum(weights, axis=-1)
    own_sums = jnp.einsum(
        "krgt,tkd->rkgd",
        weights.astype(jnp.bfloat16),
        values_flat,
        preferred_element_type=jnp.float32,
    ).reshape(row_count, head_width)
    own_maxima = jnp.transpose(maxima, (1, 0, 2)).reshape(row_count)
    own_totals = jnp.transpose(totals, (1, 0, 2)).reshape(row_count)
    merged = combine_parts(merged, (own_sums, own_maxima, own_totals))
    final_sums, final_maxima, final_totals = merged
    attended = (final_sums / final_totals[:, None]).astype(jnp.bfloat16)
    return attended.reshape(local_requests, local_heads, head_width)


def solution(mesh):
    in_specs = (
        P(("groups", "blk"), ("kv", "pair"), None),
        P(("groups", "blk", "pair"), "kv", None),
        P(("groups", "blk", "pair"), "kv", None),
        P(("groups", "blk"), "pair", "kv", None),
        P(("groups", "blk"), "pair", "kv", None),
        P(("groups", "blk")),
        P(("groups", "blk")),
    )
    out_specs = P(("groups", "blk"), ("kv", "pair"), None)
    return jax.shard_map(local, mesh=mesh, in_specs=in_specs, out_specs=out_specs, check_vma=False)
```

profile of v0, /device:TPU:0, one launch (start us, length us, event | category | flops | bytes accessed | tf_op | source)
XLA Modules:
  0.0 95.8 jit_solution(6873006721559958175)
XLA Ops:
  0.0 4.1 %constant_dynamic-slice_fusion.6 = (bf16[1024,1,2,128]{3,2,1,0:T(2,128)(2,1)}, bf16[1024,1,2,128]{3,2,1,0:T(2,128)(2,1)S(1)}, bf16[1024,1,2,128]{3,2,1,0:T(2,128)(2,1)S(1)}, bf16[1024,1,2,128]{3,2,1,0:T(2,128)(2,1)}) fusion(bf16[1024,2,2,128]{3,2,1,0:T(2,128)(2,1)} %bitcast.128, s32[]{:T(128)S(6)} %select_n.58, s32[]{:T(128)S(6)} %select_n.59, ...), kind=kLoop, calls=%fused_computation.77 | loop fusion | bytes 4194312 | tf_op jit(solution)/shard_map/jit(dynamic_index_in_dim)/dynamic_slice | solution.py:33
  6.3 3.7 %constant_dynamic-slice_fusion.2 = (bf16[2,1024,1,2,128]{4,3,2,1,0:T(2,128)(2,1)}, bf16[2,1024,1,2,128]{4,3,2,1,0:T(2,128)(2,1)S(1)}, bf16[2,1024,1,2,128]{4,3,2...) fusion(bf16[2,1024,2,2,128]{4,3,2,1,0:T(2,128)(2,1)S(1)} %bitcast.121, s32[]{:T(128)S(6)} %select_n.58, s32[]{:T(128)S(6)} %select_n.59, ...), kind=kLoop, calls=%fused_computation.73 | loop fusion | bytes 8388616 | tf_op jit(solution)/shard_map/jit(dynamic_index_in_dim)/dynamic_slice | solution.py:33
  10.1 1.2 %copy.110 = bf16[2,1024,1,2,128]{4,1,0,3,2:T(8,128)(2,1)} copy(bf16[2,1024,1,2,128]{4,3,2,1,0:T(2,128)(2,1)S(1)} %get-tuple-element.108) | data formatting | bytes 2097152 | tf_op jit(solution)/shard_map/jit(dynamic_index_in_dim)/dynamic_slice | solution.py:33
  11.7 1.2 %copy.108 = bf16[2,1024,1,2,128]{4,1,0,3,2:T(8,128)(2,1)} copy(bf16[2,1024,1,2,128]{4,3,2,1,0:T(2,128)(2,1)S(1)} %get-tuple-element.101) | data formatting | bytes 2097152 | tf_op jit(solution)/shard_map/jit(dynamic_index_in_dim)/dynamic_slice | solution.py:33
  12.9 18.0 %all_gather.3 = bf16[64,32,128]{2,1,0:T(8,128)(2,1)} all-gather(bf16[16,32,128]{2,1,0:T(8,128)(2,1)S(1)} %copy-done.5), channel_id=1, replica_groups=mesh['groups'=2,'blk'=4,'kv'=2,'pair'=2] {'blk'}, dimensions={0}, use_global_device_ids=true | all-gather | bytes 655360 | tf_op jit(solution)/shard_map/all_gather | solution.py:70
  31.1 1.1 %pad_maximum_fusion.2 = bf16[2048,2,128]{2,0,1:T(8,128)(2,1)S(1)} fusion(bf16[1024,2,128]{2,0,1:T(8,128)(2,1)} %collective-permute-done, bf16[1024,2,128]{2,0,1:T(8,128)(2,1)S(1)} %bitcast.126), kind=kLoop, calls=%fused_computation.27 | loop fusion | flops 2097152 | bytes 2097152 | tf_op jit(solution)/shard_map/concatenate | solution.py:66
  32.3 1.1 %pad_maximum_fusion.3 = bf16[2048,2,128]{2,0,1:T(8,128)(2,1)S(1)} fusion(bf16[1024,2,128]{2,0,1:T(8,128)(2,1)} %collective-permute-done.1, bf16[1024,2,128]{2,0,1:T(8,128)(2,1)S(1)} %bitcast.125), kind=kLoop, calls=%fused_computation.28 | loop fusion | flops 2097152 | bytes 2097152 | tf_op jit(solution)/shard_map/concatenate | solution.py:67
  33.4 17.2 %while.14 = (s32[]{:T(128)}, f32[4,16,2,16,128]{4,3,2,1,0:T(8,128)}, f32[4,16,2,16]{3,2,1,0:T(2,128)S(1)}, f32[4,16,2,16]{3,2,1,0:T(2,128)S(1)}, bf16[4,16,2,16,...) while((s32[]{:T(128)}, ...), condition=%wide.region_3.4_spmd, body=%wide.region_0.3_spmd.sunk | while | flops 545258496 | bytes 15671401 | solution.py:91
  33.4 1.7 %multiply_reduce_fusion.3 = (f32[2,16,16]{2,1,0:T(8,128)S(1)}, f32[2,16,16,2048]{3,2,1,0:T(8,128)S(1)}) fusion(bf16[2048,2,128]{2,0,1:T(8,128)(2,1)S(1)} %get-tuple-element.186, bf16[4,16,2,16,128]{4,3,2,1,0:T(8,128)(2,1)} %get-tuple-element.185, s32[]{:T(128)S(6)} %copy.129), kind=kOutput, calls=%fused_computation.1.clone.1 | convolution fusion | flops 270532096 | bytes 5376004 | tf_op jit(solution)/shard_map/while/body/eval_jaxpr/rkgd,tkd->krgt/dot_general | solution.py:77
  37.7 1.7 %multiply_reduce_fusion.3 = (f32[2,16,16]{2,1,0:T(8,128)S(1)}, f32[2,16,16,2048]{3,2,1,0:T(8,128)S(1)}) fusion(bf16[2048,2,128]{2,0,1:T(8,128)(2,1)S(1)} %get-tuple-element.186, bf16[4,16,2,16,128]{4,3,2,1,0:T(8,128)(2,1)} %get-tuple-element.185, s32[]{:T(128)S(6)} %copy.129), kind=kOutput, calls=%fused_computation.1.clone.1 | convolution fusion | flops 270532096 | bytes 5376004 | tf_op jit(solution)/shard_map/while/body/eval_jaxpr/rkgd,tkd->krgt/dot_general | solution.py:77
  42.0 1.7 %multiply_reduce_fusion.3 = (f32[2,16,16]{2,1,0:T(8,128)S(1)}, f32[2,16,16,2048]{3,2,1,0:T(8,128)S(1)}) fusion(bf16[2048,2,128]{2,0,1:T(8,128)(2,1)S(1)} %get-tuple-element.186, bf16[4,16,2,16,128]{4,3,2,1,0:T(8,128)(2,1)} %get-tuple-element.185, s32[]{:T(128)S(6)} %copy.129), kind=kOutput, calls=%fused_computation.1.clone.1 | convolution fusion | flops 270532096 | bytes 5376004 | tf_op jit(solution)/shard_map/while/body/eval_jaxpr/rkgd,tkd->krgt/dot_general | solution.py:77
  46.3 1.7 %multiply_reduce_fusion.3 = (f32[2,16,16]{2,1,0:T(8,128)S(1)}, f32[2,16,16,2048]{3,2,1,0:T(8,128)S(1)}) fusion(bf16[2048,2,128]{2,0,1:T(8,128)(2,1)S(1)} %get-tuple-element.186, bf16[4,16,2,16,128]{4,3,2,1,0:T(8,128)(2,1)} %get-tuple-element.185, s32[]{:T(128)S(6)} %copy.129), kind=kOutput, calls=%fused_computation.1.clone.1 | convolution fusion | flops 270532096 | bytes 5376004 | tf_op jit(solution)/shard_map/while/body/eval_jaxpr/rkgd,tkd->krgt/dot_general | solution.py:77
  51.3 5.5 %all-to-all-start.1 = ((f32[4,1,512]{2,1,0:T(1,128)}), f32[4,1,512]{2,1,0:T(1,128)S(1)}, u32[]{:S(2)}, u32[]{:S(2)}) async-start(f32[4,1,512]{2,1,0:T(1,128)} %all_to_all.26), calls=%async_computation.1 | async-start | bytes 16384 | tf_op jit(solution)/shard_map/all_to_all | solution.py:98
  57.5 4.8 %all-to-all-done.1 = f32[4,1,512]{2,1,0:T(1,128)S(1)} async-done(((f32[4,1,512]{2,1,0:T(1,128)}), f32[4,1,512]{2,1,0:T(1,128)S(1)}, u32[]{:S(2)}, u32[]{:S(2)}) %all-to-all-start.1) | async-done | bytes 8224 | tf_op jit(solution)/shard_map/all_to_all | solution.py:98
  62.4 3.2 %all-to-all-start.2 = ((f32[4,1,512]{2,1,0:T(1,128)}), f32[4,1,512]{2,1,0:T(1,128)S(1)}, u32[]{:S(2)}, u32[]{:S(2)}) async-start(f32[4,1,512]{2,1,0:T(1,128)} %all_to_all.23), calls=%async_computation.2 | async-start | bytes 16384 | tf_op jit(solution)/shard_map/all_to_all | solution.py:99
  65.8 1.4 %copy.109 = bf16[2,1024,1,2,128]{4,1,0,3,2:T(8,128)(2,1)S(1)} copy(bf16[2,1024,1,2,128]{4,3,2,1,0:T(2,128)(2,1)} %get-tuple-element.100) | data formatting | bytes 2097152 | tf_op jit(solution)/shard_map/jit(dynamic_index_in_dim)/dynamic_slice | solution.py:33
  67.4 3.8 %all-to-all-done.2 = f32[4,1,512]{2,1,0:T(1,128)S(1)} async-done(((f32[4,1,512]{2,1,0:T(1,128)}), f32[4,1,512]{2,1,0:T(1,128)S(1)}, u32[]{:S(2)}, u32[]{:S(2)}) %all-to-all-start.2) | async-done | bytes 8224 | tf_op jit(solution)/shard_map/all_to_all | solution.py:99
  71.2 3.7 %all-to-all-start = ((f32[4,512,128]{2,1,0:T(8,128)}), f32[4,512,128]{2,1,0:T(8,128)S(1)}, u32[]{:S(2)}, u32[]{:S(2)}) async-start(f32[4,512,128]{2,1,0:T(8,128)} %bitcast.130), calls=%async_computation | async-start | bytes 2097152 | tf_op jit(solution)/shard_map/all_to_all | solution.py:97
  75.0 1.4 %pad_maximum_fusion = bf16[2,2048,2,128]{3,1,0,2:T(8,128)(2,1)S(1)} fusion(bf16[2,1024,2,128]{3,1,0,2:T(8,128)(2,1)} %collective-permute-done.2, bf16[2,1024,2,128]{3,1,0,2:T(8,128)(2,1)S(1)} %bitcast.119), kind=kLoop, calls=%fused_computation.24 | loop fusion | flops 4194304 | bytes 4194304 | tf_op jit(solution)/shard_map/concatenate | solution.py:68
  76.4 1.8 %fusion.13 = (f32[2,16,16]{2,1,0:T(8,128)S(1)}, f32[2,4096,16,16]{1,3,2,0:T(8,128)S(1)}) fusion(pred[16,4096]{1,0:T(8,128)(4,1)S(1)} %compare_and_fusion, bf16[4096,2,128,1]{2,0,3,1:T(8,128)(2,1)S(1)} %bitcast.123, bf16[16,2,16,128]{3,2,1,0:T(8,128)(2,1)S(1)} %bitcast.132), kind=kOutput, calls=%fused_computation.19 | convolution fusion | flops 543161856 | bytes 10684416 | tf_op jit(solution)/shard_map/rkgd,tkd->krgt/dot_general | solution.py:119
  78.1 2.8 %fusion.14 = f32[2,16,16]{2,1,0:T(8,128)S(1)} fusion(f32[2,4096,16,16]{1,3,2,0:T(8,128)S(1)} %get-tuple-element.107, f32[2,16,16]{2,1,0:T(8,128)S(1)} %get-tuple-element.106, pred[16,4096]{1,0:T(8,128)(4,1)S(1)} %compare_and_fusion), kind=kLoop, calls=%fused_computation.20 | loop fusion | flops 10485248 | bytes 8458240 | tf_op jit(solution)/shard_map/reduce_sum | solution.py:125
  81.5 1.4 %pad_maximum_fusion.1 = bf16[2,2048,2,128]{3,1,0,2:T(8,128)(2,1)S(1)} fusion(bf16[2,1024,2,128]{3,1,0,2:T(8,128)(2,1)} %collective-permute-done.3, bf16[2,1024,2,128]{3,1,0,2:T(8,128)(2,1)S(1)} %bitcast.118), kind=kLoop, calls=%fused_computation.25 | loop fusion | flops 4194304 | bytes 4194304 | tf_op jit(solution)/shard_map/concatenate | solution.py:69
  82.8 4.9 %fusion.19 = f32[16,2,16,128]{3,2,0,1:T(8,128)S(1)} fusion(bf16[4096,2,128,1]{2,0,3,1:T(8,128)(2,1)S(1)} %bitcast.124, f32[2,4096,16,16]{1,3,2,0:T(8,128)} %copy-done, f32[2,16,16]{2,1,0:T(8,128)S(1)} %get-tuple-element.106, pred[16,4096]{1,0:T(8,128)(4,1)S(1)} %compare_and_fusion), kind=kOutput, calls=%fused_computation.26 | convolution fusion | flops 547356672 | bytes 10815488 | tf_op jit(solution)/shard_map/krgt,tkd->rkgd/dot_general | solution.py:126
  87.8 6.7 %all-to-all-done = f32[4,512,128]{2,1,0:T(8,128)S(1)} async-done(((f32[4,512,128]{2,1,0:T(8,128)}), f32[4,512,128]{2,1,0:T(8,128)S(1)}, u32[]{:S(2)}, u32[]{:S(2)}) %all-to-all-start) | async-done | bytes 1048608 | tf_op jit(solution)/shard_map/all_to_all | solution.py:97
  (65 shorter events, 17.1 us)
Async XLA Ops:
  0.0 6.3 %copy-start.1 = (bf16[2,1024,4,128]{3,2,1,0:T(4,128)(2,1)S(1)}, bf16[2,1024,4,128]{3,2,1,0:T(4,128)(2,1)}, u32[]{:S(2)}) copy-start(bf16[2,1024,4,128]{3,2,1,0:T(4,128)(2,1)} %param.13) | copy-start | bytes 6291460
  0.0 6.3 %copy-start.2 = (bf16[2,1024,4,128]{3,2,1,0:T(4,128)(2,1)S(1)}, bf16[2,1024,4,128]{3,2,1,0:T(4,128)(2,1)}, u32[]{:S(2)}) copy-start(bf16[2,1024,4,128]{3,2,1,0:T(4,128)(2,1)} %param.12) | copy-start | bytes 6291460
  5.0 26.2 %collective-permute-start = (bf16[1024,2,128]{2,0,1:T(8,128)(2,1)}, bf16[1024,2,128]{2,0,1:T(8,128)(2,1)}, u32[]{:S(2)}, u32[]{:S(2)}) collective-permute-start(bf16[1024,2,128]{2,0,1:T(8,128)(2,1)} %bitcast.103), channel_id=1, source_target_pairs={{0,1},{1,0},{2,3},{3,2},{4,5},{5,4},{6,7},{7,6},{8,9},{9,8},{10,11... | collective-permute-start | bytes 1572872 | tf_op jit(solution)/shard_map/ppermute | solution.py:12
  6.3 25.9 %collective-permute-start.1 = (bf16[1024,2,128]{2,0,1:T(8,128)(2,1)}, bf16[1024,2,128]{2,0,1:T(8,128)(2,1)}, u32[]{:S(2)}, u32[]{:S(2)}) collective-permute-start(bf16[1024,2,128]{2,0,1:T(8,128)(2,1)} %bitcast.101), channel_id=1, source_target_pairs={{0,1},{1,0},{2,3},{3,2},{4,5},{5,4},{6,7},{7,6},{8,9},{9,8},{10,11... | collective-permute-start | bytes 1572872 | tf_op jit(solution)/shard_map/ppermute | solution.py:12
  10.0 2.9 %copy-start.5 = (bf16[16,32,128]{2,1,0:T(8,128)(2,1)S(1)}, bf16[16,32,128]{2,1,0:T(8,128)(2,1)}, u32[]{:S(2)}) copy-start(bf16[16,32,128]{2,1,0:T(8,128)(2,1)} %param.9) | copy-start | bytes 393220
  10.1 20.9 %copy-start.4 = (bf16[1024,1,2,128]{3,2,1,0:T(2,128)(2,1)S(1)}, bf16[1024,1,2,128]{3,2,1,0:T(2,128)(2,1)}, u32[]{:S(2)}) copy-start(bf16[1024,1,2,128]{3,2,1,0:T(2,128)(2,1)} %get-tuple-element.102) | copy-start | bytes 1572868
  10.1 21.0 %copy-start.3 = (bf16[1024,1,2,128]{3,2,1,0:T(2,128)(2,1)S(1)}, bf16[1024,1,2,128]{3,2,1,0:T(2,128)(2,1)}, u32[]{:S(2)}) copy-start(bf16[1024,1,2,128]{3,2,1,0:T(2,128)(2,1)} %get-tuple-element.111) | copy-start | bytes 1572868
  10.1 21.0 %copy-start.7 = (s32[16]{0:T(128)S(1)}, s32[16]{0:T(128)}, u32[]{:S(2)}) copy-start(s32[16]{0:T(128)} %param.14) | copy-start | bytes 196
  11.2 63.8 %collective-permute-start.2 = (bf16[2,1024,2,128]{3,1,0,2:T(8,128)(2,1)}, bf16[2,1024,2,128]{3,1,0,2:T(8,128)(2,1)}, u32[]{:S(2)}, u32[]{:S(2)}) collective-permute-start(bf16[2,1024,2,128]{3,1,0,2:T(8,128)(2,1)} %bitcast.99), channel_id=1, source_target_pairs={{0,1},{1,0},{2,3},{3,2},{4,5},{5,4},{6,7},{7,6},{8,9},{9,8},{10,11... | collective-permute-start | bytes 3145736 | tf_op jit(solution)/shard_map/ppermute | solution.py:12
  12.9 68.6 %collective-permute-start.3 = (bf16[2,1024,2,128]{3,1,0,2:T(8,128)(2,1)}, bf16[2,1024,2,128]{3,1,0,2:T(8,128)(2,1)}, u32[]{:S(2)}, u32[]{:S(2)}) collective-permute-start(bf16[2,1024,2,128]{3,1,0,2:T(8,128)(2,1)} %bitcast.97), channel_id=1, source_target_pairs={{0,1},{1,0},{2,3},{3,2},{4,5},{5,4},{6,7},{7,6},{8,9},{9,8},{10,11... | collective-permute-start | bytes 3145736 | tf_op jit(solution)/shard_map/ppermute | solution.py:12
  33.4 32.2 %copy-start.6 = (s32[16]{0:T(128)S(1)}, s32[16]{0:T(128)}, u32[]{:S(2)}) copy-start(s32[16]{0:T(128)} %param.15) | copy-start | bytes 196
  51.3 11.1 %all-to-all-start.1 = ((f32[4,1,512]{2,1,0:T(1,128)}), f32[4,1,512]{2,1,0:T(1,128)S(1)}, u32[]{:S(2)}, u32[]{:S(2)}) async-start(f32[4,1,512]{2,1,0:T(1,128)} %all_to_all.26), calls=%async_computation.1 | async-start | bytes 16384 | tf_op jit(solution)/shard_map/all_to_all | solution.py:98
  62.4 8.8 %all-to-all-start.2 = ((f32[4,1,512]{2,1,0:T(1,128)}), f32[4,1,512]{2,1,0:T(1,128)S(1)}, u32[]{:S(2)}, u32[]{:S(2)}) async-start(f32[4,1,512]{2,1,0:T(1,128)} %all_to_all.23), calls=%async_computation.2 | async-start | bytes 16384 | tf_op jit(solution)/shard_map/all_to_all | solution.py:99
  71.2 23.4 %all-to-all-start = ((f32[4,512,128]{2,1,0:T(8,128)}), f32[4,512,128]{2,1,0:T(8,128)S(1)}, u32[]{:S(2)}, u32[]{:S(2)}) async-start(f32[4,512,128]{2,1,0:T(8,128)} %bitcast.130), calls=%async_computation | async-start | bytes 2097152 | tf_op jit(solution)/shard_map/all_to_all | solution.py:97
  78.1 3.2 %copy-start = (f32[2,4096,16,16]{1,3,2,0:T(8,128)}, f32[2,4096,16,16]{1,3,2,0:T(8,128)S(1)}, u32[]{:S(2)}) copy-start(f32[2,4096,16,16]{1,3,2,0:T(8,128)S(1)} %get-tuple-element.107) | copy-start | bytes 25165828
where the time goes:
time: 96.4 us; the launch traced here: 95.8 us
  local copies, waits for them, and re-layouts  18.9 us (20%)
  blocking collectives  18 us (19%)
  matrix products  17.4 us (18%)
  waiting for transfers between devices  15.4 us (16%)
  starting transfers between devices  13.5 us (14%)
  other arithmetic  12.4 us (13%)
    all_gather x1, blocking collectives, local(): gathered = lax.all_gather(queries, 'blk', axis=0, tiled=True)  18 us
    dynamic_slice x6, local copies, waits for them, and re-layouts, pick_index(): lax.dynamic_index_in_dim(array_in, index_value, dim_index, keepdims=False)  11.7 us
    dot_general x4, matrix products, root_partial_mine(): jnp.einsum('rkgd,tkd->krgt', query_block, keys_mine, preferred_element_ty...  6.73 us
    all_to_all x1, waiting for transfers between devices, local(): lax.all_to_all(mine_sums, 'blk', split_axis=0, concat_axis=0, tiled=True)  6.72 us
    all_to_all x1, starting transfers between devices, local(): lax.all_to_all(mine_maxima, 'blk', split_axis=0, concat_axis=0, tiled=True)  5.5 us
    dot_general x1, matrix products, local(): jnp.einsum('krgt,tkd->rkgd', weights.astype(jnp.bfloat16), values_flat, p...  4.85 us
    all_to_all x1, waiting for transfers between devices, local(): lax.all_to_all(mine_maxima, 'blk', split_axis=0, concat_axis=0, tiled=True)  4.84 us
    dot_general x4, matrix products, root_partial_mine(): jnp.einsum('krgt,tkd->rkgd', weights.astype(jnp.bfloat16), values_mine, p...  4.08 us
  transfers between devices with their start and end apart: 7, of which 3 were waited for; matrix products, arithmetic and copies ran while one was open for 42% of the time, Pallas kernels for 0%

commit v1 on v0

v1 whole, which is shorter than its diff:
```python
import functools
import math

import jax
import jax.numpy as jnp
from jax import lax
from jax.experimental import pallas as pl
from jax.experimental.pallas import tpu as pltpu
from jax.sharding import PartitionSpec as P

MESH = pl.DeviceIdType.MESH
masked_floor = -1e30
log2e = 1.4426950408889634


def kernel(
    blocks, branches,
    q_ref, rk_ref, rv_ref, bk_ref, bv_ref, rb_ref, seen_ref,
    out_ref,
    in_r, in_b, stage, mine_r, mine_b, give_r, give_b,
    q_all, p_send, p_recv, s_send, s_recv, acc_ref, max_ref, tot_ref,
    load_sem, kv_send, kv_recv, q_send, q_recv, ps_sem, pr_sem, ss_sem, sr_sem,
):
    requests, heads, width = q_ref.shape
    half = mine_r.shape[1]
    shared = 2 * half
    group = heads // half
    rows = requests * group
    root_tokens = give_r.shape[2]
    branch_tokens = give_b.shape[2]
    per_branch = branch_tokens // branches
    factor = log2e / math.sqrt(width)
    me = lax.axis_index("blk")
    core = lax.axis_index("pair")
    other = 1 - core

    loads = []
    for at, (src, dst) in enumerate(
        ((rk_ref, in_r.at[0]), (rv_ref, in_r.at[1]), (bk_ref, in_b.at[0]), (bv_ref, in_b.at[1]))
    ):
        copy = pltpu.make_async_copy(src, dst, load_sem.at[at])
        copy.start()
        loads.append(copy)

    barrier = pltpu.get_barrier_semaphore()

    @pl.loop(1, blocks)
    def _(apart):
        pl.semaphore_signal(
            barrier, inc=1, device_id={"blk": lax.rem(me + apart, blocks)}, device_id_type=MESH
        )

    pl.semaphore_signal(barrier, inc=1, device_id={"pair": other}, device_id_type=MESH)
    pl.semaphore_wait(barrier, blocks)

    def q_part(ref, i):
        return ref.at[:, pl.ds(i * group, group), :]

    def q_copy(src, slot, i, side, target):
        return pltpu.make_async_remote_copy(
            src_ref=src,
            dst_ref=q_part(q_all.at[slot], i),
            send_sem=q_send.at[side, slot, i],
            recv_sem=q_recv.at[slot, i],
            device_id={"blk": target},
            device_id_type=MESH,
        )

    for i in range(half):
        @pl.when(me + 1 < blocks)
        def _():
            q_copy(q_part(q_ref, i), me, i, 0, me + 1).start()

        @pl.when(me >= 1)
        def _():
            q_copy(q_part(q_ref, i), me, i, 1, me - 1).start()

    def forward(step):
        for i in range(half):
            @pl.when(me - step >= 0)
            def _():
                slot = me - step
                q_copy(q_part(q_ref, i), slot, i, 0, me).wait_recv()

                @pl.when(me + 1 < blocks)
                def _():
                    q_copy(q_part(q_all.at[slot], i), slot, i, 0, me + 1).start()

            @pl.when(me + step < blocks)
            def _():
                slot = me + step
                q_copy(q_part(q_ref, i), slot, i, 1, me).wait_recv()

                @pl.when(me >= 1)
                def _():
                    q_copy(q_part(q_all.at[slot], i), slot, i, 1, me - 1).start()

    def kv_copy(at, give, mine, kind, tokens):
        return pltpu.make_async_remote_copy(
            src_ref=give.at[kind],
            dst_ref=mine.at[kind, :, pl.ds(tokens, tokens), :],
            send_sem=kv_send.at[at],
            recv_sem=kv_recv.at[at],
            device_id={"pair": other},
            device_id_type=MESH,
        )

    kv_copies = (
        kv_copy(0, give_r, mine_r, 0, root_tokens),
        kv_copy(1, give_r, mine_r, 1, root_tokens),
        kv_copy(2, give_b, mine_b, 0, branch_tokens),
        kv_copy(3, give_b, mine_b, 1, branch_tokens),
    )
    span = stage.shape[0] // shared

    def spread(src, kind, mine, give, tokens):
        @pl.loop(0, tokens // span)
        def _(chunk):
            first = pl.multiple_of(chunk * (span * shared), span * shared)
            stage[...] = src[kind, pl.ds(first, span * shared), :].astype(jnp.float32)
            at = pl.multiple_of(chunk * span, span)
            for i in range(half):
                give[kind, i, pl.ds(at, span), :] = stage[
                    pl.ds(other * half + i, span, stride=shared), :
                ].astype(jnp.bfloat16)
                mine[kind, i, pl.ds(at, span), :] = stage[
                    pl.ds(core * half + i, span, stride=shared), :
                ].astype(jnp.bfloat16)

    for kind in range(2):
        loads[kind].wait()
        spread(in_r, kind, mine_r, give_r, root_tokens)
        kv_copies[kind].start()
    forward(1)
    for kind in range(2):
        loads[2 + kind].wait()
        spread(in_b, kind, mine_b, give_b, branch_tokens)
        kv_copies[2 + kind].start()

    def attend(query, keys, values, ranges):
        scores = lax.dot_general(
            query, keys, (((1,), (1,)), ((), ())), preferred_element_type=jnp.float32
        )
        if ranges is not None:
            column = lax.broadcasted_iota(jnp.int32, (group, scores.shape[1]), 1)
            visible = [(column >= low) & (column < high) for low, high in ranges]
            scores = jnp.concatenate(
                [
                    jnp.where(seen, scores[r * group : (r + 1) * group], masked_floor)
                    for r, seen in enumerate(visible)
                ],
                axis=0,
            )
        largest = jnp.max(scores, axis=-1, keepdims=True)
        weights = jnp.exp2((scores - largest) * factor)
        if ranges is not None:
            weights = jnp.where(scores > 0.5 * masked_floor, weights, 0.0)
        totals = jnp.sum(weights, axis=-1, keepdims=True)
        sums = jnp.dot(weights.astype(jnp.bfloat16), values, preferred_element_type=jnp.float32)
        return sums, largest * factor, totals

    def p_copies(slot, i, target):
        place = pl.ds(i * rows, rows)
        return (
            pltpu.make_async_remote_copy(
                src_ref=p_send.at[slot, place, :],
                dst_ref=p_recv.at[target, place, :],
                send_sem=ps_sem.at[slot, i],
                recv_sem=pr_sem.at[target, i],
                device_id={"blk": slot},
                device_id_type=MESH,
            ),
            pltpu.make_async_remote_copy(
                src_ref=s_send.at[slot, i],
                dst_ref=s_recv.at[target, i],
                send_sem=ss_sem.at[slot, i],
                recv_sem=sr_sem.at[target, i],
                device_id={"blk": slot},
                device_id_type=MESH,
            ),
        )

    kv_copies[0].wait_recv()
    kv_copies[1].wait_recv()

    @pl.loop(1, blocks)
    def _(step):
        @pl.when(step >= 2)
        def _():
            forward(step)

        @pl.loop(0, 2)
        def _(side):
            slot = me + step * (2 * side - 1)

            @pl.when((slot >= 0) & (slot < blocks))
            def _():
                for i in range(half):
                    query = q_all[slot, :, i * group : (i + 1) * group, :].reshape(rows, width)
                    sums, largest, totals = attend(query, mine_r[0, i], mine_r[1, i], None)
                    p_send[slot, i * rows : (i + 1) * rows, :] = (sums / totals).astype(
                        jnp.bfloat16
                    )
                    level = jnp.broadcast_to(largest + jnp.log(totals) * log2e, (rows, 128))
                    s_send[slot, i] = level.T[0:1, :]
                    for copy in p_copies(slot, i, me):
                        copy.start()

    kv_copies[2].wait_recv()
    kv_copies[3].wait_recv()
    ranges = ([], [])
    for r in range(requests):
        start = lax.rem(rb_ref[r], branches) * per_branch
        seen = seen_ref[r]
        for piece, owner in enumerate((core, other)):
            length = jnp.clip(seen - owner * per_branch, 0, per_branch)
            ranges[piece].append((start, start + length))
    for i in range(half):
        query = q_ref[:, i * group : (i + 1) * group, :].reshape(rows, width)
        sums, largest, totals = attend(query, mine_r[0, i], mine_r[1, i], None)
        for piece in range(2):
            place = slice(piece * branch_tokens, (piece + 1) * branch_tokens)
            more = attend(query, mine_b[0, i, place, :], mine_b[1, i, place, :], ranges[piece])
            joint = jnp.maximum(largest, more[1])
            one, two = jnp.exp2(largest - joint), jnp.exp2(more[1] - joint)
            sums = sums * one + more[0] * two
            totals = totals * one + more[2] * two
            largest = joint
        acc_ref[i] = sums
        max_ref[i] = jnp.broadcast_to(largest, (rows, width))
        tot_ref[i] = jnp.broadcast_to(totals, (rows, width))

    @pl.loop(1, blocks)
    def _(step):
        @pl.loop(0, 2)
        def _(side):
            slot = me + step * (2 * side - 1)

            @pl.when((slot >= 0) & (slot < blocks))
            def _():
                for i in range(half):
                    for copy in p_copies(slot, i, slot):
                        copy.wait_recv()
                    level = jnp.broadcast_to(s_recv[slot, i], (128, rows)).T
                    joint = jnp.maximum(max_ref[i], level)
                    one, two = jnp.exp2(max_ref[i] - joint), jnp.exp2(level - joint)
                    part = p_recv[slot, i * rows : (i + 1) * rows, :].astype(jnp.float32)
                    acc_ref[i] = acc_ref[i] * one + part * two
                    tot_ref[i] = tot_ref[i] * one + two
                    max_ref[i] = joint

    for i in range(half):
        out_ref[:, i * group : (i + 1) * group, :] = (
            (acc_ref[i] / tot_ref[i]).astype(jnp.bfloat16).reshape(requests, group, width)
        )

    for copy in kv_copies:
        copy.wait_send()

    for i in range(half):
        @pl.when(me + 1 < blocks)
        def _():
            q_copy(q_part(q_ref, i), me, i, 0, me + 1).wait_send()

        @pl.when(me >= 1)
        def _():
            q_copy(q_part(q_ref, i), me, i, 1, me - 1).wait_send()

    @pl.loop(1, blocks)
    def _(step):
        for i in range(half):
            @pl.when((me - step >= 0) & (me + 1 < blocks))
            def _():
                slot = me - step
                q_copy(q_part(q_all.at[slot], i), slot, i, 0, me + 1).wait_send()

            @pl.when((me + step < blocks) & (me >= 1))
            def _():
                slot = me + step
                q_copy(q_part(q_all.at[slot], i), slot, i, 1, me - 1).wait_send()

        slot = lax.rem(me + step, blocks)
        for i in range(half):
            for copy in p_copies(slot, i, me):
                copy.wait_send()


def local(queries, root_keys, root_values, branch_keys, branch_values, request_branch, seen_tokens):
    requests, heads, width = queries.shape
    root_tokens, shared, _ = root_keys.shape
    branches, per_branch, _, _ = branch_keys.shape
    branch_tokens = branches * per_branch
    blocks = lax.axis_size("blk")
    half = shared // lax.axis_size("pair")
    rows = requests * (heads // half)
    span = min(512, root_tokens, branch_tokens)
    bf16, f32 = jnp.bfloat16, jnp.float32
    dma = pltpu.SemaphoreType.DMA
    return pl.pallas_call(
        functools.partial(kernel, blocks, branches),
        out_shape=jax.ShapeDtypeStruct(queries.shape, bf16),
        in_specs=[pl.BlockSpec(memory_space=pltpu.VMEM)]
        + [pl.BlockSpec(memory_space=pl.ANY)] * 4
        + [pl.BlockSpec(memory_space=pltpu.SMEM)] * 2,
        out_specs=pl.BlockSpec(memory_space=pltpu.VMEM),
        scratch_shapes=[
            pltpu.VMEM((2, root_tokens * shared, width), bf16),
            pltpu.VMEM((2, branch_tokens * shared, width), bf16),
            pltpu.VMEM((span * shared, width), f32),
            pltpu.VMEM((2, half, 2 * root_tokens, width), bf16),
            pltpu.VMEM((2, half, 2 * branch_tokens, width), bf16),
            pltpu.VMEM((2, half, root_tokens, width), bf16),
            pltpu.VMEM((2, half, branch_tokens, width), bf16),
            pltpu.VMEM((blocks, requests, heads, width), bf16),
            pltpu.VMEM((blocks, half * rows, width), bf16),
            pltpu.VMEM((blocks, half * rows, width), bf16),
            pltpu.VMEM((blocks, half, 1, rows), f32),
            pltpu.VMEM((blocks, half, 1, rows), f32),
            pltpu.VMEM((half, rows, width), f32),
            pltpu.VMEM((half, rows, width), f32),
            pltpu.VMEM((half, rows, width), f32),
            dma((4,)),
            dma((4,)),
            dma((4,)),
            dma((2, blocks, half)),
            dma((blocks, half)),
            dma((blocks, half)),
            dma((blocks, half)),
            dma((blocks, half)),
            dma((blocks, half)),
        ],
        compiler_params=pltpu.CompilerParams(collective_id=0, has_side_effects=True),
        name="tree_attention",
    )(
        queries,
        root_keys.reshape(root_tokens * shared, width),
        root_values.reshape(root_tokens * shared, width),
        branch_keys.reshape(branch_tokens * shared, width),
        branch_values.reshape(branch_tokens * shared, width),
        request_branch,
        seen_tokens,
    )


def solution(mesh):
    in_specs = (
        P(("groups", "blk"), ("kv", "pair"), None),
        P(("groups", "blk", "pair"), "kv", None),
        P(("groups", "blk", "pair"), "kv", None),
        P(("groups", "blk"), "pair", "kv", None),
        P(("groups", "blk"), "pair", "kv", None),
        P(("groups", "blk")),
        P(("groups", "blk")),
    )
    out_specs = P(("groups", "blk"), ("kv", "pair"), None)
    return jax.shard_map(local, mesh=mesh, in_specs=in_specs, out_specs=out_specs, check_vma=False)
```

time: 96.4 us -> 35.1 us (0.36)
  Pallas kernels: 0 us -> 33.4 us
  blocking collectives: 18 us -> 0 us
  matrix products: 17.4 us -> 0 us
  local copies, waits for them, and re-layouts: 18.9 us -> 1.57 us
  waiting for transfers between devices: 15.4 us -> 0 us
  starting transfers between devices: 13.5 us -> 0 us
  other arithmetic: 12.4 us -> 0 us
    pallas_call x0 -> x1, Pallas kernels: none -> 33.4 us  [local(): pl.pallas_call(functools.partial(kernel, blocks, branches), out_shape=jax...]
    all_gather x1 -> x0, blocking collectives: 18 us -> none  [local(): gathered = lax.all_gather(queries, 'blk', axis=0, tiled=True)]
    dot_general x10 -> x0, matrix products: 17.4 us -> none  [the longest x4 6.73 us: root_partial_mine(): jnp.einsum('rkgd,tkd->krgt', query_block, keys_mine, preferred_element_ty...]
    all_to_all x3 -> x0, waiting for transfers between devices: 15.4 us -> none  [the longest x1 6.72 us: local(): lax.all_to_all(mine_sums, 'blk', split_axis=0, concat_axis=0, tiled=True)]
    all_to_all x3 -> x0, starting transfers between devices: 12.4 us -> none  [the longest x1 5.5 us: local(): lax.all_to_all(mine_maxima, 'blk', split_axis=0, concat_axis=0, tiled=True)]
    dynamic_slice x6 -> x0, local copies, waits for them, and re-layouts: 11.7 us -> none  [pick_index(): lax.dynamic_index_in_dim(array_in, index_value, dim_index, keepdims=False)]
    reduce_sum x7 -> x0, other arithmetic: 6.37 us -> none  [the longest x4 3.18 us: root_partial_mine(): totals = jnp.sum(weights, axis=-1)]
    concatenate x4 -> x0, other arithmetic: 4.96 us -> none  [the longest x1 1.37 us: local(): jnp.concatenate([pick_index(bkeys_split, pair_index, 2), received[2]], ax...]
  transfers between devices with their start and end apart: 7 -> 0, of which waited for: 3 -> 0; matrix products, arithmetic and copies ran while one was open for 42% -> 0% of each run, Pallas kernels for 0% -> 0%
where the time goes in v1:
time: 35.1 us; the launch traced here: 35 us
  Pallas kernels  33.4 us (95%)
  local copies, waits for them, and re-layouts  1.57 us (4%)
    pallas_call x1, Pallas kernels, local(): pl.pallas_call(functools.partial(kernel, blocks, branches), out_shape=jax...  33.4 us
    unnamed x1, local copies, waits for them, and re-layouts  1.57 us

profile of v1, /device:TPU:0, one launch (start us, length us, event | category | flops | bytes accessed | tf_op | source)
XLA Modules:
  0.0 35.0 jit_solution(6743274526007513886)
XLA Ops:
  0.0 33.4 %tree_attention.1 = bf16[16,32,128]{2,1,0:T(8,128)(2,1)} custom-call(bf16[16,32,128]{2,1,0:T(8,128)(2,1)} %q_ref.1, bf16[4096,128]{1,0:T(8,128)(2,1)} %bitcast.6, bf16[4096,128]{1,0:T(8,128)(2,1)} %bitcast.7, bf16[8192,128]{1,0:T(8,128)(2,1)} %bitcast.4, bf16[8192,128]{1,0:T(8,128)(2,1)} %bitcast.5, s32[16]{0:T(128)} %rb_ref.1, s32[16]{0:T(128)} %seen_ref.1), custom_call_target="tpu_custom_call" | custom-call | tf_op jit(solution)/shard_map/tree_attention/pallas_call | solution.py:299
  33.4 1.6 %copy.9 = bf16[16,32,128]{2,1,0:T(8,128)(2,1)} copy(bf16[16,32,128]{2,1,0:T(8,128)(2,1)} %tree_attention.1) | data formatting | bytes 262144

commit v2 on v1

--- a/solution.py
+++ b/solution.py
@@ -44,14 +44,12 @@
 
     barrier = pltpu.get_barrier_semaphore()
 
-    @pl.loop(1, blocks)
-    def _(apart):
-        pl.semaphore_signal(
-            barrier, inc=1, device_id={"blk": lax.rem(me + apart, blocks)}, device_id_type=MESH
-        )
+    for near in (me - 1, me + 1):
+        @pl.when((near >= 0) & (near < blocks))
+        def _():
+            pl.semaphore_signal(barrier, inc=1, device_id={"blk": near}, device_id_type=MESH)
 
     pl.semaphore_signal(barrier, inc=1, device_id={"pair": other}, device_id_type=MESH)
-    pl.semaphore_wait(barrier, blocks)
 
     def q_part(ref, i):
         return ref.at[:, pl.ds(i * group, group), :]
@@ -66,34 +64,19 @@
             device_id_type=MESH,
         )
 
-    for i in range(half):
-        @pl.when(me + 1 < blocks)
-        def _():
-            q_copy(q_part(q_ref, i), me, i, 0, me + 1).start()
-
-        @pl.when(me >= 1)
-        def _():
-            q_copy(q_part(q_ref, i), me, i, 1, me - 1).start()
-
     def forward(step):
         for i in range(half):
-            @pl.when(me - step >= 0)
+            @pl.when((me - step >= 0) & (me + 1 < blocks))
             def _():
                 slot = me - step
                 q_copy(q_part(q_ref, i), slot, i, 0, me).wait_recv()
-
-                @pl.when(me + 1 < blocks)
-                def _():
-                    q_copy(q_part(q_all.at[slot], i), slot, i, 0, me + 1).start()
-
-            @pl.when(me + step < blocks)
+                q_copy(q_part(q_all.at[slot], i), slot, i, 0, me + 1).start()
+
+            @pl.when((me + step < blocks) & (me >= 1))
             def _():
                 slot = me + step
                 q_copy(q_part(q_ref, i), slot, i, 1, me).wait_recv()
-
-                @pl.when(me >= 1)
-                def _():
-                    q_copy(q_part(q_all.at[slot], i), slot, i, 1, me - 1).start()
+                q_copy(q_part(q_all.at[slot], i), slot, i, 1, me - 1).start()
 
     def kv_copy(at, give, mine, kind, tokens):
         return pltpu.make_async_remote_copy(
@@ -127,15 +110,34 @@
                     pl.ds(core * half + i, span, stride=shared), :
                 ].astype(jnp.bfloat16)
 
+    @pl.when((me >= 1) & (me + 1 < blocks))
+    def _():
+        pl.semaphore_wait(barrier, 3)
+
+    @pl.when((me < 1) | (me + 1 >= blocks))
+    def _():
+        pl.semaphore_wait(barrier, 2)
+
+    for i in range(half):
+        @pl.when(me + 1 < blocks)
+        def _():
+            q_copy(q_part(q_ref, i), me, i, 0, me + 1).start()
+
+        @pl.when(me >= 1)
+        def _():
+            q_copy(q_part(q_ref, i), me, i, 1, me - 1).start()
+
     for kind in range(2):
         loads[kind].wait()
         spread(in_r, kind, mine_r, give_r, root_tokens)
+
+    for kind in range(2):
         kv_copies[kind].start()
-    forward(1)
     for kind in range(2):
         loads[2 + kind].wait()
         spread(in_b, kind, mine_b, give_b, branch_tokens)
         kv_copies[2 + kind].start()
+    forward(1)
 
     def attend(query, keys, values, ranges):
         scores = lax.dot_general(
@@ -185,17 +187,22 @@
 
     @pl.loop(1, blocks)
     def _(step):
-        @pl.when(step >= 2)
-        def _():
-            forward(step)
-
         @pl.loop(0, 2)
         def _(side):
             slot = me + step * (2 * side - 1)
+            after = me + 1 - 2 * side
+
+            @pl.when((side == 1) & (step + 1 < blocks))
+            def _():
+                forward(step + 1)
 
             @pl.when((slot >= 0) & (slot < blocks))
             def _():
                 for i in range(half):
+                    @pl.when((after < 0) | (after >= blocks))
+                    def _():
+                        q_copy(q_part(q_ref, i), slot, i, 0, me).wait_recv()
+
                     query = q_all[slot, :, i * group : (i + 1) * group, :].reshape(rows, width)
                     sums, largest, totals = attend(query, mine_r[0, i], mine_r[1, i], None)
                     p_send[slot, i * rows : (i + 1) * rows, :] = (sums / totals).astype(

time: 35.1 us -> 29.9 us (0.85)
  Pallas kernels: 33.4 us -> 28.1 us
    pallas_call x1, Pallas kernels: 33.4 us -> 28.1 us  [local(): pl.pallas_call(functools.partial(kernel, blocks, branches), out_shape=jax...]
where the time goes in v2:
time: 29.9 us; the launch traced here: 29.7 us
  Pallas kernels  28.1 us (94%)
  local copies, waits for them, and re-layouts  1.57 us (5%)
    pallas_call x1, Pallas kernels, local(): pl.pallas_call(functools.partial(kernel, blocks, branches), out_shape=jax...  28.1 us
    unnamed x1, local copies, waits for them, and re-layouts  1.57 us

profile of v2, /device:TPU:0, one launch (start us, length us, event | category | flops | bytes accessed | tf_op | source)
XLA Modules:
  0.0 29.7 jit_solution(4092220853031149334)
XLA Ops:
  0.0 28.1 %tree_attention.1 = bf16[16,32,128]{2,1,0:T(8,128)(2,1)} custom-call(bf16[16,32,128]{2,1,0:T(8,128)(2,1)} %q_ref.1, bf16[4096,128]{1,0:T(8,128)(2,1)} %bitcast.6, bf16[4096,128]{1,0:T(8,128)(2,1)} %bitcast.7, bf16[8192,128]{1,0:T(8,128)(2,1)} %bitcast.4, bf16[8192,128]{1,0:T(8,128)(2,1)} %bitcast.5, s32[16]{0:T(128)} %rb_ref.1, s32[16]{0:T(128)} %seen_ref.1), custom_call_target="tpu_custom_call" | custom-call | tf_op jit(solution)/shard_map/tree_attention/pallas_call | solution.py:306
  28.1 1.6 %copy.9 = bf16[16,32,128]{2,1,0:T(8,128)(2,1)} copy(bf16[16,32,128]{2,1,0:T(8,128)(2,1)} %tree_attention.1) | data formatting | bytes 262144

commit v3 on v2

--- a/solution.py
+++ b/solution.py
@@ -33,6 +33,7 @@
     me = lax.axis_index("blk")
     core = lax.axis_index("pair")
     other = 1 - core
+    lower = 1 - (2 * me) // blocks
 
     loads = []
     for at, (src, dst) in enumerate(
@@ -130,9 +131,8 @@
     for kind in range(2):
         loads[kind].wait()
         spread(in_r, kind, mine_r, give_r, root_tokens)
-
-    for kind in range(2):
         kv_copies[kind].start()
+
     for kind in range(2):
         loads[2 + kind].wait()
         spread(in_b, kind, mine_b, give_b, branch_tokens)
@@ -188,11 +188,12 @@
     @pl.loop(1, blocks)
     def _(step):
         @pl.loop(0, 2)
-        def _(side):
+        def _(turn):
+            side = turn + lower * (1 - 2 * turn)
             slot = me + step * (2 * side - 1)
             after = me + 1 - 2 * side
 
-            @pl.when((side == 1) & (step + 1 < blocks))
+            @pl.when((turn == 1) & (step + 1 < blocks))
             def _():
                 forward(step + 1)
 

time: 29.9 us -> 28.7 us (0.960)
  Pallas kernels: 28.1 us -> 27 us
    pallas_call x1, Pallas kernels: 28.1 us -> 27 us  [local(): pl.pallas_call(functools.partial(kernel, blocks, branches), out_shape=jax...]
where the time goes in v3:
time: 28.7 us; the launch traced here: 28.5 us
  Pallas kernels  27 us (94%)
  local copies, waits for them, and re-layouts  1.57 us (5%)
    pallas_call x1, Pallas kernels, local(): pl.pallas_call(functools.partial(kernel, blocks, branches), out_shape=jax...  27 us
    unnamed x1, local copies, waits for them, and re-layouts  1.57 us

profile of v3, /device:TPU:0, one launch (start us, length us, event | category | flops | bytes accessed | tf_op | source)
XLA Modules:
  0.0 28.5 jit_solution(9042416525132328615)
XLA Ops:
  0.0 27.0 %tree_attention.1 = bf16[16,32,128]{2,1,0:T(8,128)(2,1)} custom-call(bf16[16,32,128]{2,1,0:T(8,128)(2,1)} %q_ref.1, bf16[4096,128]{1,0:T(8,128)(2,1)} %bitcast.6, bf16[4096,128]{1,0:T(8,128)(2,1)} %bitcast.7, bf16[8192,128]{1,0:T(8,128)(2,1)} %bitcast.4, bf16[8192,128]{1,0:T(8,128)(2,1)} %bitcast.5, s32[16]{0:T(128)} %rb_ref.1, s32[16]{0:T(128)} %seen_ref.1), custom_call_target="tpu_custom_call" | custom-call | tf_op jit(solution)/shard_map/tree_attention/pallas_call | solution.py:307
  27.0 1.6 %copy.9 = bf16[16,32,128]{2,1,0:T(8,128)(2,1)} copy(bf16[16,32,128]{2,1,0:T(8,128)(2,1)} %tree_attention.1) | data formatting | bytes 262144
